TPU v7x, 256 devices: a whole 4x4x8 slice. The times are simulated.
256 devices in a mesh: seq: 32 (over y, x, core), chan: 8 (over z).
Axes of the slice: x: 4, y: 4, z: 8, core: 2. Of those that a mesh axis runs over, the one named last changes fastest.
Arguments:
- conv_in: bfloat16 [32, 512, 512], P(None, 'seq', 'chan'), may hold values from -4 to 4
- conv_gate: bfloat16 [32, 512, 512], P(None, 'seq', 'chan'), may hold values from -4 to 4
- long_filter: float32 [32, 512, 512], P(None, 'seq', 'chan'), may hold values from -1.1 to 1.1
- skip_gain: float32 [512], P('chan'), may hold values from 0.5 to 1.5
- queries: bfloat16 [32, 512, 1024], P(None, 'seq', 'chan'), may hold values from -40 to 40
- keys_in: bfloat16 [32, 512, 1024], P(None, 'seq', 'chan'), may hold values from -40 to 40
- w_value: bfloat16 [512, 1024], P(None, 'chan'), may hold values from -0.25 to 0.25
Outputs:
- conv_out: bfloat16 [32, 512, 512], P(None, 'seq', 'chan')
- attended: bfloat16 [32, 512, 1024], P(None, 'seq', 'chan')
All inputs are finite; a program needn't handle non-finite values.
Results may differ from a plain program's by a relative error of at most 0.015.
Values may be sent and summed in bfloat16 or wider, within the bound.
A program may use at most 64 MiB of HBM per device.

v0:
```python
import math
import jax
import jax.numpy as jnp
from jax import lax
from jax.sharding import PartitionSpec as P


def mixdot(form, left, right):
    return jnp.einsum(form, left, right, precision=lax.Precision.HIGHEST)


def channel_convolve(signal, long_filter):
    moved_sig, moved_tap = (
        lax.all_to_all(
            signal.astype(jnp.bfloat16), "seq", split_axis=2, concat_axis=1, tiled=True
        ).astype(signal.dtype),
        lax.all_to_all(
            long_filter.astype(jnp.bfloat16), "seq", split_axis=2, concat_axis=1, tiled=True
        ).astype(long_filter.dtype),
    )
    blocks = moved_sig.shape[0]
    length_q = moved_sig.shape[1]
    length_p = 2 * blocks
    total = length_p * length_q
    both = jnp.concatenate([moved_sig, moved_tap], axis=2).transpose(2, 0, 1)
    iota_p = jnp.arange(length_p, dtype=jnp.int32)
    iota_r = jnp.arange(blocks, dtype=jnp.int32)
    iota_q = jnp.arange(length_q, dtype=jnp.int32)
    ang_p = (iota_p[:, None] * iota_r[None, :] % length_p).astype(jnp.float32) * (
        2.0 * math.pi / length_p
    )
    ang_q = (iota_q[:, None] * iota_q[None, :] % length_q).astype(jnp.float32) * (
        2.0 * math.pi / length_q
    )
    ang_t = (iota_p[:, None] * iota_q[None, :] % total).astype(jnp.float32) * (
        2.0 * math.pi / total
    )
    cos_p = jnp.cos(ang_p)
    sin_p = jnp.sin(ang_p)
    cos_q = jnp.cos(ang_q)
    sin_q = jnp.sin(ang_q)
    cos_t = jnp.cos(ang_t)
    sin_t = jnp.sin(ang_t)
    first_re = mixdot("kn,cnq->ckq", cos_p, both)
    first_im = -mixdot("kn,cnq->ckq", sin_p, both)
    tw_re = first_re * cos_t + first_im * sin_t
    tw_im = first_im * cos_t - first_re * sin_t
    spec_re = mixdot("ckq,qm->ckm", tw_re, cos_q) + mixdot("ckq,qm->ckm", tw_im, sin_q)
    spec_im = mixdot("ckq,qm->ckm", tw_im, cos_q) - mixdot("ckq,qm->ckm", tw_re, sin_q)
    half_count = both.shape[0] // 2
    sig_re = spec_re[:half_count]
    sig_im = spec_im[:half_count]
    tap_re = spec_re[half_count:]
    tap_im = spec_im[half_count:]
    prod_re = sig_re * tap_re - sig_im * tap_im
    prod_im = sig_re * tap_im + sig_im * tap_re
    inner_re = mixdot("ckm,mq->ckq", prod_re, cos_q) - mixdot("ckm,mq->ckq", prod_im, sin_q)
    inner_im = mixdot("ckm,mq->ckq", prod_im, cos_q) + mixdot("ckm,mq->ckq", prod_re, sin_q)
    turned_re = inner_re * cos_t - inner_im * sin_t
    turned_im = inner_im * cos_t + inner_re * sin_t
    result = (mixdot("kn,ckq->cnq", cos_p, turned_re) - mixdot("kn,ckq->cnq", sin_p, turned_im)) * (
        1.0 / total
    )
    return lax.all_to_all(
        result.transpose(1, 2, 0).astype(jnp.bfloat16),
        "seq",
        split_axis=1,
        concat_axis=2,
        tiled=True,
    ).astype(jnp.float32)


def body(conv_in, conv_gate, long_filter, skip_gain, queries, keys_in, w_value):
    blocks, slab_rows, channels = conv_in.shape
    my_index = lax.axis_index("seq")
    tokens = blocks * slab_rows
    signal = conv_in.astype(jnp.float32)
    positions = (
        jnp.arange(blocks, dtype=jnp.int32)[:, None] * tokens
        + my_index * slab_rows
        + jnp.arange(slab_rows, dtype=jnp.int32)[None, :]
    )
    convolved = channel_convolve(signal, long_filter)
    mixed = (convolved + skip_gain * signal) * conv_gate.astype(jnp.float32)
    conv_out = mixed.astype(jnp.bfloat16)
    head_size = w_value.shape[1]
    piece = lax.all_gather(conv_out, "chan", axis=2, tiled=True)
    piece_width = piece.shape[2]
    value_sum = jnp.dot(
        piece.reshape(tokens, piece_width), w_value, preferred_element_type=jnp.float32
    )
    values = value_sum.astype(jnp.bfloat16).reshape(blocks, slab_rows, head_size)
    query_rows = queries.reshape(tokens, head_size)
    query_pos = positions.reshape(tokens)
    score_scale = 1.0 / math.sqrt(head_size)
    empty_state = (
        jnp.full((tokens,), -1e30, jnp.float32),
        jnp.zeros((tokens,), jnp.float32),
        jnp.zeros((tokens, head_size), jnp.float32),
    )
    key_piece = lax.all_gather(keys_in, "seq", axis=1, tiled=True)
    value_piece = lax.all_gather(values, "seq", axis=1, tiled=True)
    width_now = key_piece.shape[1]
    target = max(1, 1024 // blocks)
    step_size = 1
    for candidate in range(min(width_now, target), 0, -1):
        step_size = candidate
        break

    def key_step(step_index, current):
        row_best, row_total, row_accum = current
        offset = step_index * step_size
        key_block = lax.dynamic_slice_in_dim(key_piece, offset, step_size, 1).reshape(
            blocks * step_size, head_size
        )
        value_block = lax.dynamic_slice_in_dim(value_piece, offset, step_size, 1).reshape(
            blocks * step_size, head_size
        )
        key_pos = (
            jnp.arange(blocks, dtype=jnp.int32)[:, None] * tokens
            + offset
            + jnp.arange(step_size, dtype=jnp.int32)[None, :]
        ).reshape(blocks * step_size)
        scores = (
            jnp.einsum("qd,kd->qk", query_rows, key_block, preferred_element_type=jnp.float32)
            * score_scale
        )
        allowed = key_pos[None, :] <= query_pos[:, None]
        scores = jnp.where(allowed, scores, -1e30)
        new_best = jnp.maximum(row_best, jnp.max(scores, axis=1))
        factor = jnp.exp(row_best - new_best)
        weights = jnp.where(allowed, jnp.exp(scores - new_best[:, None]), 0.0)
        row_total = row_total * factor + jnp.sum(weights, axis=1)
        row_accum = row_accum * factor[:, None] + jnp.dot(
            weights.astype(jnp.bfloat16), value_block, preferred_element_type=jnp.float32
        )
        return (new_best, row_total, row_accum)

    final_best, final_total, final_accum = lax.fori_loop(
        0, width_now // step_size, key_step, empty_state
    )
    attended = (
        (final_accum / final_total[:, None])
        .astype(jnp.bfloat16)
        .reshape(blocks, slab_rows, head_size)
    )
    return (conv_out, attended)


def solution(mesh):
    return jax.shard_map(
        body,
        mesh=mesh,
        in_specs=(
            P(None, "seq", "chan"),
            P(None, "seq", "chan"),
            P(None, "seq", "chan"),
            P("chan"),
            P(None, "seq", "chan"),
            P(None, "seq", "chan"),
            P(None, "chan"),
        ),
        out_specs=(P(None, "seq", "chan"), P(None, "seq", "chan")),
        check_vma=False,
    )
```

profile of v0, /device:TPU:1, one launch (start us, length us, event | category | flops | bytes accessed | tf_op | source)
XLA Modules:
  0.0 245.0 jit_solution(10891590349229744156)
XLA Ops:
  10.0 8.6 %all-to-all-start.1 = ((bf16[32,2,512]{2,1,0:T(2,128)(2,1)}), bf16[32,2,512]{2,1,0:T(2,128)(2,1)S(1)}, u32[]{:S(2)}, u32[]{:S(2)}) async-start(bf16[32,2,512]{2,1,0:T(2,128)(2,1)} %reshape.130), calls=%async_computation.1 | async-start | bytes 131072 | tf_op jit(solution)/shard_map/all_to_all | solution.py:17
  18.6 1.2 copy.75
  20.7 5.2 %all-to-all-done.1 = bf16[32,2,512]{2,1,0:T(2,128)(2,1)S(1)} async-done(((bf16[32,2,512]{2,1,0:T(2,128)(2,1)}), bf16[32,2,512]{2,1,0:T(2,128)(2,1)S(1)}, u32[]{:S(2)}, u32[]{:S(2)}) %all-to-all-start.1) | async-done | bytes 65568 | tf_op jit(solution)/shard_map/all_to_all | solution.py:17
  26.0 3.9 %all-to-all-start = ((bf16[32,2,512]{2,1,0:T(2,128)(2,1)}), bf16[32,2,512]{2,1,0:T(2,128)(2,1)S(1)}, u32[]{:S(2)}, u32[]{:S(2)}) async-start(bf16[32,2,512]{2,1,0:T(2,128)(2,1)} %reshape.132), calls=%async_computation | async-start | bytes 131072 | tf_op jit(solution)/shard_map/all_to_all | solution.py:14
  30.7 6.6 %all-to-all-done = bf16[32,2,512]{2,1,0:T(2,128)(2,1)S(1)} async-done(((bf16[32,2,512]{2,1,0:T(2,128)(2,1)}), bf16[32,2,512]{2,1,0:T(2,128)(2,1)S(1)}, u32[]{:S(2)}, u32[]{:S(2)}) %all-to-all-start) | async-done | bytes 65568 | tf_op jit(solution)/shard_map/all_to_all | solution.py:14
  38.7 5.4 %fusion.30 = f32[4,64,512]{2,1,0:T(8,128)S(1)} fusion(f32[4,64,512]{2,1,0:T(8,128)S(1)} %convolution_bitcast_fusion, f32[4,64,512]{2,1,0:T(8,128)S(1)} %fusion.15, f32[64,512]{1,0:T(8,128)S(1)} %get-tuple-element.210, f32[64,512]{1,0:T(8,128)S(1)} %get-tuple-element.211), kind=kOutput, calls=%fused_computation.51 | convolution fusion | flops 809369600 | bytes 1835008 | tf_op jit(solution)/shard_map/ckq,qm->ckm/dot_general | solution.py:9
  44.1 5.4 %fusion.32 = f32[4,64,512]{2,1,0:T(8,128)S(1)} fusion(f32[4,64,512]{2,1,0:T(8,128)S(1)} %fusion.15, f32[4,64,512]{2,1,0:T(8,128)S(1)} %convolution_bitcast_fusion, f32[64,512]{1,0:T(8,128)S(1)} %get-tuple-element.210, f32[64,512]{1,0:T(8,128)S(1)} %get-tuple-element.211), kind=kOutput, calls=%fused_computation.53 | convolution fusion | flops 809369600 | bytes 1835008 | tf_op jit(solution)/shard_map/ckq,qm->ckm/dot_general | solution.py:9
  49.5 5.4 %convolution_subtract_fusion = f32[4,64,512]{2,1,0:T(8,128)S(1)} fusion(f32[4,64,512]{2,1,0:T(8,128)S(1)} %fusion.30, f32[4,64,512]{2,1,0:T(8,128)S(1)} %fusion.15, f32[4,64,512]{2,1,0:T(8,128)S(1)} %convolution_bitcast_fusion, f32[64,512]{1,0:T(8,128)S(1)} %get-tuple-element.210, f32[64,512]{1,0:T(8,128)S(1)} %get-tuple-element.211), kind=kOutput, calls=%fused_computation.28 | convolution fusion | flops 809500672 | bytes 2359296 | tf_op jit(solution)/shard_map/ckq,qm->ckm/dot_general | solution.py:9
  54.9 5.6 %convolution_add_fusion.1 = f32[4,64,512]{2,1,0:T(8,128)S(1)} fusion(f32[4,64,512]{2,1,0:T(8,128)S(1)} %fusion.32, f32[4,64,512]{2,1,0:T(8,128)S(1)} %convolution_bitcast_fusion, f32[4,64,512]{2,1,0:T(8,128)S(1)} %fusion.15, f32[64,512]{1,0:T(8,128)S(1)} %get-tuple-element.210, f32[64,512]{1,0:T(8,128)S(1)} %get-tuple-element.211), kind=kOutput, calls=%fused_computation.29 | convolution fusion | flops 809500672 | bytes 2359296 | tf_op jit(solution)/shard_map/ckq,qm->ckm/dot_general | solution.py:9
  60.6 4.9 %fusion.28 = f32[2,64,512]{2,1,0:T(8,128)S(1)} fusion(f32[2,64,512]{2,1,0:T(8,128)S(1)} %get-tuple-element.208), kind=kOutput, calls=%fused_computation.49 | convolution fusion | flops 406323200 | bytes 524288 | tf_op jit(solution)/shard_map/ckm,mq->ckq/dot_general | solution.py:9
  65.5 4.9 %fusion.26 = f32[2,64,512]{2,1,0:T(8,128)S(1)} fusion(f32[2,64,512]{2,1,0:T(8,128)S(1)} %get-tuple-element.209), kind=kOutput, calls=%fused_computation.47 | convolution fusion | flops 406323200 | bytes 524288 | tf_op jit(solution)/shard_map/ckm,mq->ckq/dot_general | solution.py:9
  70.4 4.9 %convolution_subtract_fusion.1 = f32[2,64,512]{2,1,0:T(8,128)S(1)} fusion(f32[2,64,512]{2,1,0:T(8,128)S(1)} %fusion.28, f32[2,64,512]{2,1,0:T(8,128)S(1)} %get-tuple-element.209), kind=kOutput, calls=%fused_computation.34 | convolution fusion | flops 406388736 | bytes 786432 | tf_op jit(solution)/shard_map/ckm,mq->ckq/dot_general | solution.py:9
  75.2 5.1 %convolution_add_fusion.2 = f32[2,64,512]{2,1,0:T(8,128)S(1)} fusion(f32[2,64,512]{2,1,0:T(8,128)S(1)} %fusion.26, f32[2,64,512]{2,1,0:T(8,128)S(1)} %get-tuple-element.208), kind=kOutput, calls=%fused_computation.33 | convolution fusion | flops 406388736 | bytes 786432 | tf_op jit(solution)/shard_map/ckm,mq->ckq/dot_general | solution.py:9
  82.2 3.9 %all-to-all-start.2 = ((bf16[32,2,512]{2,1,0:T(2,128)(2,1)}), bf16[32,2,512]{2,1,0:T(2,128)(2,1)S(1)}, u32[]{:S(2)}, u32[]{:S(2)}) async-start(bf16[32,2,512]{2,1,0:T(2,128)(2,1)} %reshape.134), calls=%async_computation.2 | async-start | bytes 131072 | tf_op jit(solution)/shard_map/all_to_all | solution.py:64
  86.5 7.1 %all-to-all-done.2 = bf16[32,2,512]{2,1,0:T(2,128)(2,1)S(1)} async-done(((bf16[32,2,512]{2,1,0:T(2,128)(2,1)}), bf16[32,2,512]{2,1,0:T(2,128)(2,1)S(1)}, u32[]{:S(2)}, u32[]{:S(2)}) %all-to-all-start.2) | async-done | bytes 65568 | tf_op jit(solution)/shard_map/all_to_all | solution.py:64
  94.1 28.8 %all_gather.10 = bf16[32,16,512]{0,1,2:T(8,128)(2,1)S(1)} all-gather(bf16[32,16,64]{0,1,2:T(8,128)(2,1)S(1)} %fusion.38), channel_id=1, replica_groups=mesh['seq'=32,'chan'=8] {'chan'}, dimensions={2}, use_global_device_ids=true | all-gather | bytes 589824 | tf_op jit(solution)/shard_map/all_gather | solution.py:87
  123.0 2.2 copy.86
  127.2 53.7 %all-gather.5.cloned.1.call-done = bf16[32,512,128]{2,1,0:T(8,128)(2,1)} async-done(((bf16[32,16,128]{2,1,0:T(8,128)(2,1)}), bf16[32,512,128]{2,1,0:T(8,128)(2,1)}) %all-gather.5.cloned.1.call-update) | async-done | bytes 4194320 | tf_op jit(solution)/shard_map/all_gather | solution.py:102
  180.8 56.5 %while.18 = (s32[]{:T(128)}, f32[512]{0:T(512)S(1)}, f32[512]{0:T(512)S(1)}, f32[512,128]{1,0:T(8,128)S(1)}, bf16[32,512,128]{2,1,0:T(8,128)(2,1)}, /*index=5*/b...) while((s32[]{:T(128)}, f32[512]{0:T(512)S(1)}, ...), condition=%wide.region_3.4_spmd.clone, body=%wide.region_0.3_spmd.clone.sunk | while | flops 277024832 | bytes 8589887 | solution.py:139
  181.1 1.1 constant_dynamic-slice_fusion.3
  183.3 1.0 convolution_add_fusion.4
  184.7 1.1 constant_dynamic-slice_fusion.3
  186.9 1.0 convolution_add_fusion.4
  188.2 1.1 constant_dynamic-slice_fusion.3
  190.4 1.0 convolution_add_fusion.4
  191.7 1.1 constant_dynamic-slice_fusion.3
  193.9 1.0 convolution_add_fusion.4
  195.3 1.1 constant_dynamic-slice_fusion.3
  197.5 1.0 convolution_add_fusion.4
  198.8 1.1 constant_dynamic-slice_fusion.3
  201.0 1.0 convolution_add_fusion.4
  202.3 1.1 constant_dynamic-slice_fusion.3
  205.9 1.1 constant_dynamic-slice_fusion.3
  208.1 1.0 convolution_add_fusion.4
  209.4 1.1 constant_dynamic-slice_fusion.3
  212.9 1.1 constant_dynamic-slice_fusion.3
  215.1 1.0 convolution_add_fusion.4
  216.4 1.1 constant_dynamic-slice_fusion.3
  218.7 1.0 convolution_add_fusion.4
  220.0 1.1 constant_dynamic-slice_fusion.3
  222.2 1.0 convolution_add_fusion.4
  223.5 1.1 constant_dynamic-slice_fusion.3
  225.7 1.0 convolution_add_fusion.4
  227.0 1.1 constant_dynamic-slice_fusion.3
  229.2 1.0 convolution_add_fusion.4
  230.6 1.1 constant_dynamic-slice_fusion.3
  234.1 1.1 constant_dynamic-slice_fusion.3
  236.3 1.0 convolution_add_fusion.4
  (207 shorter events, 37.0 us)
Async XLA Ops:
  7.2 118.0 %copy-start = (bf16[512,128]{1,0:T(8,128)(2,1)S(1)}, bf16[512,128]{1,0:T(8,128)(2,1)}, u32[]{:S(2)}) copy-start(bf16[512,128]{1,0:T(8,128)(2,1)} %param.15) | copy-start | bytes 393220
  7.2 120.0 %all-gather.3.cloned.1.call-start = ((), (), s32[]{:S(2)}) async-start(), calls=%async_computation.3 | async-start | bytes 4325376 | tf_op jit(solution)/shard_map/all_gather | solution.py:101
  10.0 15.9 %all-to-all-start.1 = ((bf16[32,2,512]{2,1,0:T(2,128)(2,1)}), bf16[32,2,512]{2,1,0:T(2,128)(2,1)S(1)}, u32[]{:S(2)}, u32[]{:S(2)}) async-start(bf16[32,2,512]{2,1,0:T(2,128)(2,1)} %reshape.130), calls=%async_computation.1 | async-start | bytes 131072 | tf_op jit(solution)/shard_map/all_to_all | solution.py:17
  26.0 11.3 %all-to-all-start = ((bf16[32,2,512]{2,1,0:T(2,128)(2,1)}), bf16[32,2,512]{2,1,0:T(2,128)(2,1)S(1)}, u32[]{:S(2)}, u32[]{:S(2)}) async-start(bf16[32,2,512]{2,1,0:T(2,128)(2,1)} %reshape.132), calls=%async_computation | async-start | bytes 131072 | tf_op jit(solution)/shard_map/all_to_all | solution.py:14
  80.3 5.9 %copy-start.1 = (bf16[32,16,64]{2,1,0:T(8,128)(2,1)S(1)}, bf16[32,16,64]{2,1,0:T(8,128)(2,1)}, u32[]{:S(2)}) copy-start(bf16[32,16,64]{2,1,0:T(8,128)(2,1)} %param.10) | copy-start | bytes 196612
  81.2 12.8 %copy-start.2 = (f32[64]{0:T(128)S(1)}, f32[64]{0:T(128)}, u32[]{:S(2)}) copy-start(f32[64]{0:T(128)} %param.12) | copy-start | bytes 772
  82.2 11.4 %all-to-all-start.2 = ((bf16[32,2,512]{2,1,0:T(2,128)(2,1)}), bf16[32,2,512]{2,1,0:T(2,128)(2,1)S(1)}, u32[]{:S(2)}, u32[]{:S(2)}) async-start(bf16[32,2,512]{2,1,0:T(2,128)(2,1)} %reshape.134), calls=%async_computation.2 | async-start | bytes 131072 | tf_op jit(solution)/shard_map/all_to_all | solution.py:64
  86.2 94.6 %all-gather.5.cloned.1.call-start = ((), (), s32[]{:S(2)}) async-start(), calls=%async_computation.4 | async-start | bytes 4325376 | tf_op jit(solution)/shard_map/all_gather | solution.py:102
  123.0 57.8 %copy-start.3 = (bf16[32,16,128]{2,1,0:T(8,128)(2,1)S(1)}, bf16[32,16,128]{2,1,0:T(8,128)(2,1)}, u32[]{:S(2)}) copy-start(bf16[32,16,128]{2,1,0:T(8,128)(2,1)} %param.13) | copy-start | bytes 393220
Sparse Core Ops, SparseCore 0:
  10.5 58.7 all-gather.2
  126.3 54.5 all-gather.4
where the time goes:
time: 246 us; the launch traced here: 245 us
  waiting for transfers between devices  73.2 us (30%)
  matrix products  67.3 us (27%)
  blocking collectives  28.8 us (12%)
  local copies, waits for them, and re-layouts  28.4 us (12%)
  starting transfers between devices  16.5 us (7%)
  other arithmetic  15.3 us (6%)
  between operations  14.4 us (6%)
    all_gather x1, waiting for transfers between devices, body(): value_piece = lax.all_gather(values, 'seq', axis=1, tiled=True)  53.7 us
    dot_general x12, matrix products, mixdot(): return jnp.einsum(form, left, right, precision=lax.Precision.HIGHEST)  43.3 us
    all_gather x1, blocking collectives, body(): piece = lax.all_gather(conv_out, 'chan', axis=2, tiled=True)  28.8 us
    dynamic_slice x16, local copies, waits for them, and re-layouts, key_step(): lax.dynamic_slice_in_dim(value_piece, offset, step_size, 1)  17.2 us
    dot_general x16, matrix products, key_step(): jnp.dot(weights.astype(jnp.bfloat16), value_block, preferred_element_type...  15.7 us
    reduce_sum x16, other arithmetic, key_step(): row_total = row_total * factor + jnp.sum(weights, axis=1)  9.97 us
    all_to_all x1, starting transfers between devices, channel_convolve(): lax.all_to_all(long_filter.astype(jnp.bfloat16), 'seq', split_axis=2, con...  8.59 us
    dot_general x16, matrix products, key_step(): jnp.einsum('qd,kd->qk', query_rows, key_block, preferred_element_type=jnp...  7.38 us
  transfers between devices with their start and end apart: 5, of which 4 were waited for; matrix products, arithmetic and copies ran while one was open for 22% of the time, Pallas kernels for 0%

commit v1 on v0

--- a/solution.py
+++ b/solution.py
@@ -84,7 +84,10 @@
     mixed = (convolved + skip_gain * signal) * conv_gate.astype(jnp.float32)
     conv_out = mixed.astype(jnp.bfloat16)
     head_size = w_value.shape[1]
-    piece = lax.all_gather(conv_out, "chan", axis=2, tiled=True)
+    f_next = lax.axis_size("chan")
+    part_next = jnp.stack(f_next * [conv_out])
+    local_next = lax.all_to_all(part_next, "chan", 0, 0)
+    piece = jnp.concatenate(local_next, 2)
     piece_width = piece.shape[2]
     value_sum = jnp.dot(
         piece.reshape(tokens, piece_width), w_value, preferred_element_type=jnp.float32

time: 246 us -> 237 us (0.963)
  waiting for transfers between devices: 73.2 us -> 68 us
  blocking collectives: 28.8 us -> 24.6 us
    all_gather x1 -> x0, blocking collectives: 28.8 us -> none  [body(): piece = lax.all_gather(conv_out, 'chan', axis=2, tiled=True)]
    all_to_all x0 -> x1, blocking collectives: none -> 24.6 us  [body(): local_next = lax.all_to_all(part_next, 'chan', 0, 0)]
    all_gather x1, waiting for transfers between devices: 53.7 us -> 48.4 us  [body(): value_piece = lax.all_gather(values, 'seq', axis=1, tiled=True)]
    unnamed x17 -> x21, local copies, waits for them, and re-layouts: 5.61 us -> 6.33 us
  transfers between devices with their start and end apart: 5 -> 5, of which waited for: 4 -> 4; matrix products, arithmetic and copies ran while one was open for 22% -> 23% of each run, Pallas kernels for 0% -> 0%
where the time goes in v1:
time: 237 us; the launch traced here: 236 us
  waiting for transfers between devices  68 us (29%)
  matrix products  67.3 us (28%)
  local copies, waits for them, and re-layouts  28.9 us (12%)
  blocking collectives  24.6 us (10%)
  starting transfers between devices  16.5 us (7%)
  other arithmetic  15.3 us (6%)
  between operations  14.4 us (6%)
    all_gather x1, waiting for transfers between devices, body(): value_piece = lax.all_gather(values, 'seq', axis=1, tiled=True)  48.4 us
    dot_general x12, matrix products, mixdot(): return jnp.einsum(form, left, right, precision=lax.Precision.HIGHEST)  43.3 us
    all_to_all x1, blocking collectives, body(): local_next = lax.all_to_all(part_next, 'chan', 0, 0)  24.6 us
    dynamic_slice x16, local copies, waits for them, and re-layouts, key_step(): lax.dynamic_slice_in_dim(value_piece, offset, step_size, 1)  17.2 us
    dot_general x16, matrix products, key_step(): jnp.dot(weights.astype(jnp.bfloat16), value_block, preferred_element_type...  15.7 us
    reduce_sum x16, other arithmetic, key_step(): row_total = row_total * factor + jnp.sum(weights, axis=1)  9.97 us
    all_to_all x1, starting transfers between devices, channel_convolve(): lax.all_to_all(long_filter.astype(jnp.bfloat16), 'seq', split_axis=2, con...  8.59 us
    dot_general x16, matrix products, key_step(): jnp.einsum('qd,kd->qk', query_rows, key_block, preferred_element_type=jnp...  7.35 us
  transfers between devices with their start and end apart: 5, of which 4 were waited for; matrix products, arithmetic and copies ran while one was open for 23% of the time, Pallas kernels for 0%

profile of v1, /device:TPU:1, one launch (start us, length us, event | category | flops | bytes accessed | tf_op | source)
XLA Modules:
  0.0 236.0 jit_solution(656207928193739853)
XLA Ops:
  10.0 8.6 %all-to-all-start.1 = ((bf16[32,2,512]{2,1,0:T(2,128)(2,1)}), bf16[32,2,512]{2,1,0:T(2,128)(2,1)S(1)}, u32[]{:S(2)}, u32[]{:S(2)}) async-start(bf16[32,2,512]{2,1,0:T(2,128)(2,1)} %reshape.132), calls=%async_computation.1 | async-start | bytes 131072 | tf_op jit(solution)/shard_map/all_to_all | solution.py:17
  18.6 1.2 copy.67
  20.7 5.2 %all-to-all-done.1 = bf16[32,2,512]{2,1,0:T(2,128)(2,1)S(1)} async-done(((bf16[32,2,512]{2,1,0:T(2,128)(2,1)}), bf16[32,2,512]{2,1,0:T(2,128)(2,1)S(1)}, u32[]{:S(2)}, u32[]{:S(2)}) %all-to-all-start.1) | async-done | bytes 65568 | tf_op jit(solution)/shard_map/all_to_all | solution.py:17
  26.0 3.9 %all-to-all-start = ((bf16[32,2,512]{2,1,0:T(2,128)(2,1)}), bf16[32,2,512]{2,1,0:T(2,128)(2,1)S(1)}, u32[]{:S(2)}, u32[]{:S(2)}) async-start(bf16[32,2,512]{2,1,0:T(2,128)(2,1)} %reshape.134), calls=%async_computation | async-start | bytes 131072 | tf_op jit(solution)/shard_map/all_to_all | solution.py:14
  30.7 6.6 %all-to-all-done = bf16[32,2,512]{2,1,0:T(2,128)(2,1)S(1)} async-done(((bf16[32,2,512]{2,1,0:T(2,128)(2,1)}), bf16[32,2,512]{2,1,0:T(2,128)(2,1)S(1)}, u32[]{:S(2)}, u32[]{:S(2)}) %all-to-all-start) | async-done | bytes 65568 | tf_op jit(solution)/shard_map/all_to_all | solution.py:14
  38.7 5.4 %fusion.30 = f32[4,64,512]{2,1,0:T(8,128)S(1)} fusion(f32[4,64,512]{2,1,0:T(8,128)S(1)} %convolution_bitcast_fusion, f32[4,64,512]{2,1,0:T(8,128)S(1)} %fusion.15, f32[64,512]{1,0:T(8,128)S(1)} %get-tuple-element.208, f32[64,512]{1,0:T(8,128)S(1)} %get-tuple-element.209), kind=kOutput, calls=%fused_computation.51 | convolution fusion | flops 809369600 | bytes 1835008 | tf_op jit(solution)/shard_map/ckq,qm->ckm/dot_general | solution.py:9
  44.1 5.4 %fusion.32 = f32[4,64,512]{2,1,0:T(8,128)S(1)} fusion(f32[4,64,512]{2,1,0:T(8,128)S(1)} %fusion.15, f32[4,64,512]{2,1,0:T(8,128)S(1)} %convolution_bitcast_fusion, f32[64,512]{1,0:T(8,128)S(1)} %get-tuple-element.208, f32[64,512]{1,0:T(8,128)S(1)} %get-tuple-element.209), kind=kOutput, calls=%fused_computation.53 | convolution fusion | flops 809369600 | bytes 1835008 | tf_op jit(solution)/shard_map/ckq,qm->ckm/dot_general | solution.py:9
  49.5 5.4 %convolution_subtract_fusion = f32[4,64,512]{2,1,0:T(8,128)S(1)} fusion(f32[4,64,512]{2,1,0:T(8,128)S(1)} %fusion.30, f32[4,64,512]{2,1,0:T(8,128)S(1)} %fusion.15, f32[4,64,512]{2,1,0:T(8,128)S(1)} %convolution_bitcast_fusion, f32[64,512]{1,0:T(8,128)S(1)} %get-tuple-element.208, f32[64,512]{1,0:T(8,128)S(1)} %get-tuple-element.209), kind=kOutput, calls=%fused_computation.28 | convolution fusion | flops 809500672 | bytes 2359296 | tf_op jit(solution)/shard_map/ckq,qm->ckm/dot_general | solution.py:9
  54.9 5.6 %convolution_add_fusion.1 = f32[4,64,512]{2,1,0:T(8,128)S(1)} fusion(f32[4,64,512]{2,1,0:T(8,128)S(1)} %fusion.32, f32[4,64,512]{2,1,0:T(8,128)S(1)} %convolution_bitcast_fusion, f32[4,64,512]{2,1,0:T(8,128)S(1)} %fusion.15, f32[64,512]{1,0:T(8,128)S(1)} %get-tuple-element.208, f32[64,512]{1,0:T(8,128)S(1)} %get-tuple-element.209), kind=kOutput, calls=%fused_computation.29 | convolution fusion | flops 809500672 | bytes 2359296 | tf_op jit(solution)/shard_map/ckq,qm->ckm/dot_general | solution.py:9
  60.6 4.9 %fusion.28 = f32[2,64,512]{2,1,0:T(8,128)S(1)} fusion(f32[2,64,512]{2,1,0:T(8,128)S(1)} %get-tuple-element.206), kind=kOutput, calls=%fused_computation.49 | convolution fusion | flops 406323200 | bytes 524288 | tf_op jit(solution)/shard_map/ckm,mq->ckq/dot_general | solution.py:9
  65.5 4.9 %fusion.26 = f32[2,64,512]{2,1,0:T(8,128)S(1)} fusion(f32[2,64,512]{2,1,0:T(8,128)S(1)} %get-tuple-element.207), kind=kOutput, calls=%fused_computation.47 | convolution fusion | flops 406323200 | bytes 524288 | tf_op jit(solution)/shard_map/ckm,mq->ckq/dot_general | solution.py:9
  70.4 4.9 %convolution_subtract_fusion.1 = f32[2,64,512]{2,1,0:T(8,128)S(1)} fusion(f32[2,64,512]{2,1,0:T(8,128)S(1)} %fusion.28, f32[2,64,512]{2,1,0:T(8,128)S(1)} %get-tuple-element.207), kind=kOutput, calls=%fused_computation.34 | convolution fusion | flops 406388736 | bytes 786432 | tf_op jit(solution)/shard_map/ckm,mq->ckq/dot_general | solution.py:9
  75.2 5.1 %convolution_add_fusion.2 = f32[2,64,512]{2,1,0:T(8,128)S(1)} fusion(f32[2,64,512]{2,1,0:T(8,128)S(1)} %fusion.26, f32[2,64,512]{2,1,0:T(8,128)S(1)} %get-tuple-element.206), kind=kOutput, calls=%fused_computation.33 | convolution fusion | flops 406388736 | bytes 786432 | tf_op jit(solution)/shard_map/ckm,mq->ckq/dot_general | solution.py:9
  82.2 3.9 %all-to-all-start.2 = ((bf16[32,2,512]{2,1,0:T(2,128)(2,1)}), bf16[32,2,512]{2,1,0:T(2,128)(2,1)S(1)}, u32[]{:S(2)}, u32[]{:S(2)}) async-start(bf16[32,2,512]{2,1,0:T(2,128)(2,1)} %reshape.136), calls=%async_computation.2 | async-start | bytes 131072 | tf_op jit(solution)/shard_map/all_to_all | solution.py:64
  86.5 7.1 %all-to-all-done.2 = bf16[32,2,512]{2,1,0:T(2,128)(2,1)S(1)} async-done(((bf16[32,2,512]{2,1,0:T(2,128)(2,1)}), bf16[32,2,512]{2,1,0:T(2,128)(2,1)S(1)}, u32[]{:S(2)}, u32[]{:S(2)}) %all-to-all-start.2) | async-done | bytes 65568 | tf_op jit(solution)/shard_map/all_to_all | solution.py:64
  95.3 24.6 %all_to_all.32 = bf16[8,2,16384]{2,1,0:T(2,128)(2,1)S(1)} all-to-all(bf16[8,2,16384]{2,1,0:T(2,128)(2,1)S(1)} %reshape.138), channel_id=1, replica_groups=mesh['seq'=32,'chan'=8] {'chan'}, dimensions={0} | all-to-all | bytes 1048576 | tf_op jit(solution)/shard_map/all_to_all | solution.py:89
  120.6 1.2 copy.79
  123.5 48.4 %all-gather.5.cloned.1.call-done = bf16[32,512,128]{2,1,0:T(8,128)(2,1)} async-done(((bf16[32,16,128]{2,1,0:T(8,128)(2,1)}), bf16[32,512,128]{2,1,0:T(8,128)(2,1)}) %all-gather.5.cloned.1.call-update) | async-done | bytes 4194320 | tf_op jit(solution)/shard_map/all_gather | solution.py:105
  171.9 56.5 %while.18 = (s32[]{:T(128)}, f32[512]{0:T(512)S(1)}, f32[512]{0:T(512)S(1)}, f32[512,128]{1,0:T(8,128)S(1)}, bf16[32,512,128]{2,1,0:T(8,128)(2,1)}, /*index=5*/b...) while((s32[]{:T(128)}, f32[512]{0:T(512)S(1)}, ...), condition=%wide.region_3.4_spmd.clone, body=%wide.region_0.3_spmd.clone.sunk | while | flops 277024832 | bytes 8589887 | solution.py:142
  172.2 1.1 constant_dynamic-slice_fusion.3
  174.4 1.0 convolution_add_fusion.4
  175.7 1.1 constant_dynamic-slice_fusion.3
  177.9 1.0 convolution_add_fusion.4
  179.3 1.1 constant_dynamic-slice_fusion.3
  182.8 1.1 constant_dynamic-slice_fusion.3
  185.0 1.0 convolution_add_fusion.4
  186.3 1.1 constant_dynamic-slice_fusion.3
  188.5 1.0 convolution_add_fusion.4
  189.8 1.1 constant_dynamic-slice_fusion.3
  193.4 1.1 constant_dynamic-slice_fusion.3
  195.6 1.0 convolution_add_fusion.4
  196.9 1.1 constant_dynamic-slice_fusion.3
  199.1 1.0 convolution_add_fusion.4
  200.4 1.1 constant_dynamic-slice_fusion.3
  202.6 1.0 convolution_add_fusion.4
  204.0 1.1 constant_dynamic-slice_fusion.3
  206.2 1.0 convolution_add_fusion.4
  207.5 1.1 constant_dynamic-slice_fusion.3
  209.7 1.0 convolution_add_fusion.4
  211.0 1.1 constant_dynamic-slice_fusion.3
  213.2 1.0 convolution_add_fusion.4
  214.6 1.1 constant_dynamic-slice_fusion.3
  216.8 1.0 convolution_add_fusion.4
  218.1 1.1 constant_dynamic-slice_fusion.3
  220.3 1.0 convolution_add_fusion.4
  221.6 1.1 constant_dynamic-slice_fusion.3
  225.2 1.1 constant_dynamic-slice_fusion.3
  227.4 1.0 convolution_add_fusion.4
  (213 shorter events, 38.4 us)
Async XLA Ops:
  7.2 115.2 %copy-start = (bf16[512,128]{1,0:T(8,128)(2,1)S(1)}, bf16[512,128]{1,0:T(8,128)(2,1)}, u32[]{:S(2)}) copy-start(bf16[512,128]{1,0:T(8,128)(2,1)} %param.15) | copy-start | bytes 393220
  7.2 116.3 %all-gather.3.cloned.1.call-start = ((), (), s32[]{:S(2)}) async-start(), calls=%async_computation.4 | async-start | bytes 4325376 | tf_op jit(solution)/shard_map/all_gather | solution.py:104
  10.0 15.9 %all-to-all-start.1 = ((bf16[32,2,512]{2,1,0:T(2,128)(2,1)}), bf16[32,2,512]{2,1,0:T(2,128)(2,1)S(1)}, u32[]{:S(2)}, u32[]{:S(2)}) async-start(bf16[32,2,512]{2,1,0:T(2,128)(2,1)} %reshape.132), calls=%async_computation.1 | async-start | bytes 131072 | tf_op jit(solution)/shard_map/all_to_all | solution.py:17
  26.0 11.3 %all-to-all-start = ((bf16[32,2,512]{2,1,0:T(2,128)(2,1)}), bf16[32,2,512]{2,1,0:T(2,128)(2,1)S(1)}, u32[]{:S(2)}, u32[]{:S(2)}) async-start(bf16[32,2,512]{2,1,0:T(2,128)(2,1)} %reshape.134), calls=%async_computation | async-start | bytes 131072 | tf_op jit(solution)/shard_map/all_to_all | solution.py:14
  80.3 5.9 %copy-start.2 = (bf16[32,16,64]{2,1,0:T(8,128)(2,1)S(1)}, bf16[32,16,64]{2,1,0:T(8,128)(2,1)}, u32[]{:S(2)}) copy-start(bf16[32,16,64]{2,1,0:T(8,128)(2,1)} %param.10) | copy-start | bytes 196612
  81.2 12.8 %copy-start.3 = (f32[64]{0:T(128)S(1)}, f32[64]{0:T(128)}, u32[]{:S(2)}) copy-start(f32[64]{0:T(128)} %param.12) | copy-start | bytes 772
  82.2 11.4 %all-to-all-start.2 = ((bf16[32,2,512]{2,1,0:T(2,128)(2,1)}), bf16[32,2,512]{2,1,0:T(2,128)(2,1)S(1)}, u32[]{:S(2)}, u32[]{:S(2)}) async-start(bf16[32,2,512]{2,1,0:T(2,128)(2,1)} %reshape.136), calls=%async_computation.2 | async-start | bytes 131072 | tf_op jit(solution)/shard_map/all_to_all | solution.py:64
  86.2 85.7 %all-gather.5.cloned.1.call-start = ((), (), s32[]{:S(2)}) async-start(), calls=%async_computation.5 | async-start | bytes 4325376 | tf_op jit(solution)/shard_map/all_gather | solution.py:105
  94.5 26.1 %copy-start.1 = (bf16[32,16,64]{2,1,0:T(8,128)(2,1)}, bf16[32,16,64]{2,1,0:T(8,128)(2,1)S(1)}, u32[]{:S(2)}) copy-start(bf16[32,16,64]{2,1,0:T(8,128)(2,1)S(1)} %copy.80) | copy-start | bytes 196612
  120.5 51.3 %copy-start.4 = (bf16[32,16,128]{2,1,0:T(8,128)(2,1)S(1)}, bf16[32,16,128]{2,1,0:T(8,128)(2,1)}, u32[]{:S(2)}) copy-start(bf16[32,16,128]{2,1,0:T(8,128)(2,1)} %param.13) | copy-start | bytes 393220
Sparse Core Ops, SparseCore 0:
  10.5 58.7 all-gather.2
  123.5 48.3 all-gather.4
